TPU v7x, 32 devices: a whole 2x2x4 slice. The times are simulated.
32 devices in a mesh: zone: 4 (over y, x), dev: 8 (over z, core).
Axes of the slice: x: 2, y: 2, z: 4, core: 2. Of those that a mesh axis runs over, the one named last changes fastest.
Arguments:
- quad_weight: float32 [16384, 128], P(('zone', 'dev')), may hold values from 0.002 to 0.014
- param_coords: float32 [16384, 4, 128], P(('zone', 'dev')), may hold values from -1 to 1
- slave_points: float32 [16384, 3, 128], P(('zone', 'dev')), may hold values from -6 to 6
- slave_normals: float32 [16384, 3, 128], P(('zone', 'dev')), may hold values from -1 to 1, as said below
- block_owner: int32 [16384, 1], P(('zone', 'dev')), may hold values from 0 to 7; in each aligned block of 128 rows (0 to 127, 128 to 255, ...) at most 16 rows name the same one
- block_patch: int32 [16384], P(('zone', 'dev')), may hold values from 0 to 8191
- block_count: int32 [32, 4], P(('zone', 'dev')), may hold values from 1 to 128, as said below
- active_flags: int32 [4, 16384], P(None, ('zone', 'dev')), may hold values 0 or 1
- normal_mult: float32 [4, 16384], P(None, ('zone', 'dev')), may hold values from 0.5 to 4
- tangent_mult: float32 [12, 16384], P(None, ('zone', 'dev')), may hold values from -6 to 6
- master_patch: float32 [12, 262144], P(None, ('zone', 'dev')), may hold values from -6 to 6
Outputs:
- mortar_d: float32 [16, 16384], P(None, ('zone', 'dev'))
- mortar_m: float32 [16, 16384], P(None, ('zone', 'dev'))
- gap_lin: float32 [48, 16384], P(None, ('zone', 'dev'))
- gap_res: float32 [4, 16384], P(None, ('zone', 'dev'))
- cone_res: float32 [12, 16384], P(None, ('zone', 'dev'))
Inputs may be any that keep to these rules, and one draw needn't show every extreme that they name: Device q's live blocks toward group k are the first block_count[q, k] of its 128 slots for k; in every draw each device fills all 128 slots toward one group, the same group for all devices of one dev index. `slave_normals`: every normal has unit length. `block_owner`: in each aligned block of 128 slots (one device toward one group) no owner is named by more than 16 slots.
All inputs are finite; a program needn't handle non-finite values. No bound on the sum of `active_flags` on one device may be relied on, other than what follows from the above.
Results may differ from a plain program's by a relative error of at most 0.0003.
Values sent between devices are 32-bit elements; how exact they have to be, the bound alone decides.
A program may use at most 320 MiB of HBM per device.

v0:
```python
import jax
import jax.numpy as jnp
from jax import lax
from jax.sharding import PartitionSpec as P

BUCKET = 16
friction_coef = 0.3
newton_scale = 4.0


def bilinear(first, second):
    return jnp.stack(
        [
            0.25 * (1.0 - first) * (1.0 - second),
            0.25 * (1.0 + first) * (1.0 - second),
            0.25 * (1.0 + first) * (1.0 + second),
            0.25 * (1.0 - first) * (1.0 + second),
        ],
        axis=0,
    )


def slave_terms(weight, coords):
    shape_s = bilinear(coords[:, 2], coords[:, 3])
    weighted = weight[None] * shape_s
    return jnp.sum(weighted[:, None] * shape_s[None], axis=-1).reshape(16, -1)


def master_terms(weight, coords, points, normals, corners):
    shape_s = bilinear(coords[:, 2], coords[:, 3])
    shape_m = bilinear(coords[:, 0], coords[:, 1])
    weighted = weight[None] * shape_s
    paired = weighted[:, None] * shape_m[None]
    mortar_m = jnp.sum(paired, axis=-1).reshape(16, -1)
    diffs = []
    for direction in range(3):
        position = jnp.sum(shape_m * corners[4 * direction : 4 * direction + 4][:, :, None], axis=0)
        diffs.append(position - points[:, direction])
    gap_point = normals[:, 0] * diffs[0] + normals[:, 1] * diffs[1] + normals[:, 2] * diffs[2]
    wgap = jnp.sum(weighted * gap_point[None], axis=-1)
    slips = [
        jnp.sum(weighted * (diffs[direction] - normals[:, direction] * gap_point)[None], axis=-1)
        for direction in range(3)
    ]
    lins = [
        jnp.sum(paired * normals[:, direction][None, None], axis=-1).reshape(16, -1)
        for direction in range(3)
    ]
    return (mortar_m, wgap, jnp.concatenate(slips, axis=0), jnp.concatenate(lins, axis=0))


def residuals(wgap, wslip, active, normal_mult, tangent_mult):
    radius = friction_coef * normal_mult
    trial = tangent_mult + newton_scale * wslip
    length = jnp.sqrt(trial[0:4] * trial[0:4] + trial[4:8] * trial[4:8] + trial[8:12] * trial[8:12])
    factor = radius / jnp.maximum(radius, length)
    factor_all = jnp.concatenate([factor, factor, factor], axis=0)
    active_all = jnp.concatenate([active, active, active], axis=0)
    cone = jnp.where(active_all == 1, tangent_mult - factor_all * trial, tangent_mult)
    gap = jnp.where(active == 1, wgap, normal_mult)
    return (gap, cone)


def live_slots(counts, slots, groups):
    cap = slots // groups
    index = jnp.arange(slots, dtype=jnp.int32)
    group_of = index // cap
    per_slot = jnp.sum(
        jnp.where(
            group_of[:, None] == jnp.arange(groups, dtype=jnp.int32)[None, :], counts[None, :], 0
        ),
        axis=1,
    )
    return index % cap < per_slot


def lookup(owner, offset, master_patch):
    count = owner.shape[0]
    peers = lax.axis_size("dev")
    sources = lax.axis_size("zone")
    width = sources * BUCKET
    block = count // sources
    peer_index = jnp.arange(peers, dtype=jnp.int32)
    hits = (owner.reshape(sources, block)[:, :, None] == peer_index[None, None, :]).astype(
        jnp.int32
    )
    before = jnp.cumsum(hits, axis=1) - hits
    rank = jnp.sum(before * hits, axis=2)
    position = (jnp.arange(sources, dtype=jnp.int32)[:, None] * BUCKET + rank).reshape(count)
    table = jnp.zeros((peers, width), jnp.int32).at[owner, position].set(offset)
    found = jnp.take(
        master_patch, lax.all_to_all(table, "dev", split_axis=0, concat_axis=0, tiled=True), axis=1
    )
    replies = lax.all_to_all(found, "dev", split_axis=1, concat_axis=1, tiled=True)
    flat = replies.reshape(12, peers * width)
    return jnp.take(flat, owner * width + position, axis=1)


def local(
    quad_weight,
    param_coords,
    slave_points,
    slave_normals,
    block_owner,
    block_patch,
    block_count,
    active_flags,
    normal_mult,
    tangent_mult,
    master_patch,
):
    groups = lax.axis_size("zone")
    slots = quad_weight.shape[0]
    mortar_d = slave_terms(quad_weight, param_coords)
    owner_ids = block_owner[:, 0]
    asked_owner, asked_patch = (
        lax.all_to_all(owner_ids, "zone", split_axis=0, concat_axis=0, tiled=True),
        lax.all_to_all(block_patch, "zone", split_axis=0, concat_axis=0, tiled=True),
    )
    found = lookup(asked_owner, asked_patch, master_patch)
    corners = lax.all_to_all(found, "zone", split_axis=1, concat_axis=1, tiled=True)
    back_m, back_gap, back_slip, back_lin = master_terms(
        quad_weight, param_coords, slave_points, slave_normals, corners
    )
    gap, cone = residuals(back_gap, back_slip, active_flags, normal_mult, tangent_mult)
    live = live_slots(block_count[0], slots, groups)[None]
    return (
        jnp.where(live, mortar_d, 0.0),
        jnp.where(live, back_m, 0.0),
        jnp.where(live, back_lin, 0.0),
        jnp.where(live, gap, 0.0),
        jnp.where(live, cone, 0.0),
    )


def solution(mesh):
    placed = (
        P(("zone", "dev"), None),
        P(("zone", "dev"), None, None),
        P(("zone", "dev"), None, None),
        P(("zone", "dev"), None, None),
        P(("zone", "dev"), None),
        P(("zone", "dev")),
        P(("zone", "dev"), None),
        P(None, ("zone", "dev")),
        P(None, ("zone", "dev")),
        P(None, ("zone", "dev")),
        P(None, ("zone", "dev")),
    )
    return jax.shard_map(
        local,
        mesh=mesh,
        in_specs=placed,
        out_specs=(
            P(None, ("zone", "dev")),
            P(None, ("zone", "dev")),
            P(None, ("zone", "dev")),
            P(None, ("zone", "dev")),
            P(None, ("zone", "dev")),
        ),
        check_vma=False,
    )
```

profile of v0, /device:TPU:0, one launch (start us, length us, event | category | flops | bytes accessed | tf_op | source)
XLA Modules:
  0.0 147.0 jit_solution(7890981640103569913)
XLA Ops:
  0.6 5.2 %all-to-all-start = ((s32[4,128,1]{1,2,0:T(1,128)}), s32[4,128,1]{1,2,0:T(1,128)S(1)}, u32[]{:S(2)}, u32[]{:S(2)}) async-start(s32[4,128,1]{1,2,0:T(1,128)} %bitcast.121), calls=%async_computation | async-start | bytes 4096 | tf_op jit(solution)/shard_map/all_to_all | solution.py:117
  5.8 3.4 %fusion.17 = (f32[512,1,128]{2,1,0:T(1,128)S(1)}, f32[512,1,128]{2,1,0:T(1,128)S(1)}, f32[512,1,128]{2,1,0:T(1,128)S(1)}, f32[512,1,128]{2,1,0:T(1,128)S(1)}) fusion(f32[512,4,128]{2,1,0:T(4,128)} %param.12), kind=kLoop, calls=%fused_computation.99 | loop fusion | bytes 2097152 | tf_op jit(solution)/shard_map/slice | solution.py:24
  9.2 1.2 slice_bitcast_fusion.1
  10.4 0.0 copy-start.7
  10.4 1.1 multiply_bitcast_fusion.3
  11.5 0.8 multiply_bitcast_fusion.7
  12.3 0.0 all-to-all-done
  12.3 4.2 %all-to-all-start.1 = ((s32[4,128,1]{1,2,0:T(1,128)}), s32[4,128,1]{1,2,0:T(1,128)S(1)}, u32[]{:S(2)}, u32[]{:S(2)}) async-start(s32[4,128,1]{1,2,0:T(1,128)} %bitcast.18), calls=%async_computation.1 | async-start | bytes 4096 | tf_op jit(solution)/shard_map/all_to_all | solution.py:118
  16.5 0.1 fusion.3
  16.6 0.3 reduce_window_sum.11
  16.9 0.2 select_reduce_fusion
  17.1 0.1 compare_and_fusion.1
  17.2 3.8 %all-to-all-done.1 = s32[4,128,1]{1,2,0:T(1,128)S(1)} async-done(((s32[4,128,1]{1,2,0:T(1,128)}), s32[4,128,1]{1,2,0:T(1,128)S(1)}, u32[]{:S(2)}, u32[]{:S(2)}) %all-to-all-start.1) | async-done | bytes 2080 | tf_op jit(solution)/shard_map/all_to_all | solution.py:118
  21.0 0.6 broadcast_in_dim.120
  21.6 76.9 %scatter_fusion = s32[8,64]{1,0:T(8,128)} fusion(s32[8,64]{1,0:T(8,128)} %broadcast_in_dim.120, s32[512]{0:T(512)S(1)} %bitcast.104, s32[512]{0:T(512)S(1)} %bitcast.118), kind=kCustom, calls=%fused_computation.2 | custom fusion | bytes 10240 | tf_op jit(solution)/shard_map/scatter | solution.py:90
  98.5 4.9 %all-to-all-start.2 = ((s32[8,1,64]{2,1,0:T(1,128)}), s32[8,1,64]{2,1,0:T(1,128)S(1)}, u32[]{:S(2)}, u32[]{:S(2)}) async-start(s32[8,1,64]{2,1,0:T(1,128)} %bitcast.21), calls=%async_computation.2 | async-start | bytes 8192 | tf_op jit(solution)/shard_map/all_to_all | solution.py:92
  103.4 0.0 copy-done.7
  103.4 0.1 select_reduce_fusion.1
  103.5 3.6 %copy.70 = f32[12,8192]{0,1:T(8,128)} copy(f32[12,8192]{1,0:T(8,128)} %param.21) | data formatting | bytes 786432 | tf_op args[10]
  107.1 1.8 %all-to-all-done.2 = s32[8,1,64]{2,1,0:T(1,128)S(1)} async-done(((s32[8,1,64]{2,1,0:T(1,128)}), s32[8,1,64]{2,1,0:T(1,128)S(1)}, u32[]{:S(2)}, u32[]{:S(2)}) %all-to-all-start.2) | async-done | bytes 2080 | tf_op jit(solution)/shard_map/all_to_all | solution.py:92
  108.9 0.1 reshape.572
  108.9 3.2 %gather_fusion = f32[512,12]{1,0:T(8,128)S(1)} fusion(f32[12,8192]{0,1:T(8,128)} %copy.70, s32[1024]{0:T(1024)S(1)} %pad_clamp_fusion.1), kind=kCustom, calls=%fused_computation | custom fusion | bytes 51200 | tf_op jit(solution)/shard_map/jit(_take)/gather | solution.py:91
  112.2 0.1 copy.71
  112.3 0.7 reshape.593
  113.0 3.3 %all-to-all-start.3 = ((f32[8,1,768]{2,1,0:T(1,128)}), f32[8,1,768]{2,1,0:T(1,128)S(1)}, u32[]{:S(2)}, u32[]{:S(2)}) async-start(f32[8,1,768]{2,1,0:T(1,128)} %reshape.593), calls=%async_computation.3 | async-start | bytes 49152 | tf_op jit(solution)/shard_map/all_to_all | solution.py:94
  116.4 5.7 %all-to-all-done.3 = f32[8,1,768]{2,1,0:T(1,128)S(1)} async-done(((f32[8,1,768]{2,1,0:T(1,128)}), f32[8,1,768]{2,1,0:T(1,128)S(1)}, u32[]{:S(2)}, u32[]{:S(2)}) %all-to-all-start.3) | async-done | bytes 24608 | tf_op jit(solution)/shard_map/all_to_all | solution.py:94
  122.1 0.5 broadcast.412
  122.6 0.7 reduce
  123.3 0.1 reshape.594
  123.4 0.1 copy.72
  123.5 1.6 %gather_fusion.1 = f32[512,12]{1,0:T(8,128)} fusion(f32[12,512]{0,1:T(8,128)S(1)} %bitcast.105, s32[1024]{0:T(1024)S(1)} %pad_clamp_fusion), kind=kCustom, calls=%fused_computation.1 | custom fusion | bytes 51200 | tf_op jit(solution)/shard_map/jit(_take)/gather | solution.py:96
  125.2 1.1 copy.73
  126.2 0.6 broadcast_select_fusion
  126.9 3.3 %all-to-all-start.4 = ((f32[12,4,128]{2,0,1:T(8,128)}), f32[12,4,128]{2,0,1:T(8,128)S(1)}, u32[]{:S(2)}, u32[]{:S(2)}) async-start(f32[12,4,128]{2,0,1:T(8,128)} %broadcast_select_fusion), calls=%async_computation.4 | async-start | bytes 65536 | tf_op jit(solution)/shard_map/all_to_all | solution.py:121
  130.2 4.7 %all-to-all-done.4 = f32[12,4,128]{2,0,1:T(8,128)S(1)} async-done(((f32[12,4,128]{2,0,1:T(8,128)}), f32[12,4,128]{2,0,1:T(8,128)S(1)}, u32[]{:S(2)}, u32[]{:S(2)}) %all-to-all-start.4) | async-done | bytes 24608 | tf_op jit(solution)/shard_map/all_to_all | solution.py:121
  134.9 2.2 %multiply_reduce_fusion.6 = (f32[512,128]{1,0:T(8,128)S(1)}, f32[512,128]{1,0:T(8,128)S(1)}, f32[512,128]{1,0:T(8,128)S(1)}, f32[4,512,128]{2,1,0:T(8,128)S(1)}) fusion(f32[4,512]{1,0:T(4,128)S(1)} %get-tuple-element.42, f32[1,512,128]{2,1,0:T(8,128)} %get-tuple-element.39, f32[1,512,128]{2,1,0:T(8,128)} %get-tuple-element.40, ...), kind=kLoop, calls=%fused_computation.17 | loop fusion | flops 2162688 | bytes 2908160 | tf_op jit(solution)/shard_map/reduce_sum | solution.py:37
  137.1 0.0 copy-start.4
  137.1 0.2 multiply_subtract_fusion.1
  137.3 0.0 copy-start.5
  137.3 0.0 copy-start.6
  137.3 0.1 multiply_subtract_fusion
  137.4 1.3 multiply_reduce_fusion.4
  138.7 0.0 copy-done.4
  138.8 0.6 maximum_divide_fusion
  139.4 0.6 fusion.4
  140.0 5.6 %fusion = (f32[4,4,512]{2,1,0:T(4,128)S(1)}, f32[4,4,512]{2,1,0:T(4,128)S(1)}, f32[4,4,512]{2,1,0:T(4,128)S(1)}, f32[4,4,512]{2,1,0:T(4,128)S(1)}, f32[4,4,512]{2,1,0:T(4,128)S(1)}) fusion(f32[512,128]{1,0:T(8,128)S(1)} %get-tuple-element.31, f32[4,512,128]{2,1,0:T(8,128)S(1)} %get-tuple-element.29, f32[4,512,128]{2,1,0:T(8,128)S(1)} %get-tuple-element.17, ...), kind=kLoop, calls=%fused_computation.7 | loop fusion | flops 10444800 | bytes 4096000 | tf_op jit(solution)/shard_map/reduce_sum | solution.py:46
  145.7 0.6 broadcast_select_fusion.1
  146.4 0.6 maximum_select_fusion
  (26 shorter events, 0.2 us)
Async XLA Ops:
  0.6 11.6 %all-to-all-start = ((s32[4,128,1]{1,2,0:T(1,128)}), s32[4,128,1]{1,2,0:T(1,128)S(1)}, u32[]{:S(2)}, u32[]{:S(2)}) async-start(s32[4,128,1]{1,2,0:T(1,128)} %bitcast.121), calls=%async_computation | async-start | bytes 4096 | tf_op jit(solution)/shard_map/all_to_all | solution.py:117
  10.4 93.0 %copy-start.7 = (s32[1,4]{1,0:T(1,128)S(1)}, s32[1,4]{1,0:T(1,128)}, u32[]{:S(2)}) copy-start(s32[1,4]{1,0:T(1,128)} %param.17) | copy-start | bytes 52
  12.3 8.8 %all-to-all-start.1 = ((s32[4,128,1]{1,2,0:T(1,128)}), s32[4,128,1]{1,2,0:T(1,128)S(1)}, u32[]{:S(2)}, u32[]{:S(2)}) async-start(s32[4,128,1]{1,2,0:T(1,128)} %bitcast.18), calls=%async_computation.1 | async-start | bytes 4096 | tf_op jit(solution)/shard_map/all_to_all | solution.py:118
  98.5 10.4 %all-to-all-start.2 = ((s32[8,1,64]{2,1,0:T(1,128)}), s32[8,1,64]{2,1,0:T(1,128)S(1)}, u32[]{:S(2)}, u32[]{:S(2)}) async-start(s32[8,1,64]{2,1,0:T(1,128)} %bitcast.21), calls=%async_computation.2 | async-start | bytes 8192 | tf_op jit(solution)/shard_map/all_to_all | solution.py:92
  103.5 33.6 %copy-start = (f32[512,3,128]{2,0,1:T(8,128)S(1)}, f32[512,3,128]{2,0,1:T(8,128)}, u32[]{:S(2)}) copy-start(f32[512,3,128]{2,0,1:T(8,128)} %param.14) | copy-start | bytes 2359300
  103.5 33.6 %copy-start.1 = (f32[512,3,128]{2,0,1:T(8,128)S(1)}, f32[512,3,128]{2,0,1:T(8,128)}, u32[]{:S(2)}) copy-start(f32[512,3,128]{2,0,1:T(8,128)} %param.13) | copy-start | bytes 2359300
  113.0 9.0 %all-to-all-start.3 = ((f32[8,1,768]{2,1,0:T(1,128)}), f32[8,1,768]{2,1,0:T(1,128)S(1)}, u32[]{:S(2)}, u32[]{:S(2)}) async-start(f32[8,1,768]{2,1,0:T(1,128)} %reshape.593), calls=%async_computation.3 | async-start | bytes 49152 | tf_op jit(solution)/shard_map/all_to_all | solution.py:94
  126.2 11.2 %copy-start.2 = (f32[1,512,128]{2,1,0:T(8,128)S(1)}, f32[1,512,128]{2,1,0:T(8,128)}, u32[]{:S(2)}) copy-start(f32[1,512,128]{2,1,0:T(8,128)} %get-tuple-element.36) | copy-start | bytes 786436
  126.9 8.0 %all-to-all-start.4 = ((f32[12,4,128]{2,0,1:T(8,128)}), f32[12,4,128]{2,0,1:T(8,128)S(1)}, u32[]{:S(2)}, u32[]{:S(2)}) async-start(f32[12,4,128]{2,0,1:T(8,128)} %broadcast_select_fusion), calls=%async_computation.4 | async-start | bytes 65536 | tf_op jit(solution)/shard_map/all_to_all | solution.py:121
  134.9 2.6 %copy-start.3 = (f32[512,128]{1,0:T(8,128)S(1)}, f32[512,128]{1,0:T(8,128)}, u32[]{:S(2)}) copy-start(f32[512,128]{1,0:T(8,128)} %param.11) | copy-start | bytes 786436
  137.1 1.6 %copy-start.4 = (f32[12,512]{1,0:T(8,128)S(1)}, f32[12,512]{1,0:T(8,128)}, u32[]{:S(2)}) copy-start(f32[12,512]{1,0:T(8,128)} %param.20) | copy-start | bytes 73732
  137.3 1.5 %copy-start.5 = (s32[4,512]{1,0:T(4,128)S(1)}, s32[4,512]{1,0:T(4,128)}, u32[]{:S(2)}) copy-start(s32[4,512]{1,0:T(4,128)} %param.18) | copy-start | bytes 24580
  137.3 1.5 %copy-start.6 = (f32[4,512]{1,0:T(4,128)S(1)}, f32[4,512]{1,0:T(4,128)}, u32[]{:S(2)}) copy-start(f32[4,512]{1,0:T(4,128)} %param.19) | copy-start | bytes 24580
where the time goes:
time: 149 us; the launch traced here: 147 us
  local copies, waits for them, and re-layouts  93.4 us (63%)
  starting transfers between devices  20.9 us (14%)
  other arithmetic  16 us (11%)
  waiting for transfers between devices  16 us (11%)
    scatter x1, local copies, waits for them, and re-layouts, lookup(): table = jnp.zeros((peers, width), jnp.int32).at[owner, position].set(offset)  76.9 us
    all_to_all x1, waiting for transfers between devices, lookup(): lax.all_to_all(found, 'dev', split_axis=1, concat_axis=1, tiled=True)  5.68 us
    reduce_sum x1, other arithmetic, master_terms(): jnp.sum(paired * normals[:, direction][None, None], axis=-1).reshape(16, -1)  5.61 us
    all_to_all x1, starting transfers between devices, local(): lax.all_to_all(owner_ids, 'zone', split_axis=0, concat_axis=0, tiled=True)  5.18 us
    all_to_all x1, starting transfers between devices, lookup(): lax.all_to_all(table, 'dev', split_axis=0, concat_axis=0, tiled=True)  4.88 us
    all_to_all x1, waiting for transfers between devices, local(): lax.all_to_all(found, 'zone', split_axis=1, concat_axis=1, tiled=True)  4.71 us
    unnamed x19, local copies, waits for them, and re-layouts  4.45 us
    all_to_all x1, starting transfers between devices, local(): lax.all_to_all(block_patch, 'zone', split_axis=0, concat_axis=0, tiled=True)  4.19 us
  transfers between devices with their start and end apart: 5, of which 4 were waited for; matrix products, arithmetic and copies ran while one was open for 7% of the time, Pallas kernels for 0%

commit v1 on v0

--- a/solution.py
+++ b/solution.py
@@ -91,7 +91,18 @@
     found = jnp.take(
         master_patch, lax.all_to_all(table, "dev", split_axis=0, concat_axis=0, tiled=True), axis=1
     )
-    replies = lax.all_to_all(found, "dev", split_axis=1, concat_axis=1, tiled=True)
+    ways, here = (lax.axis_size("dev"), lax.axis_index("dev"))
+    width_2 = found.shape[1] // ways
+    shape = list(found.shape)
+    shape[1] = width_2
+    height = shape[1]
+    shape[1] = height * ways
+    replies = jnp.zeros(shape, found.dtype)
+    for mask in range(ways):
+        part = lax.dynamic_slice_in_dim(found, (here ^ mask) * width_2, width_2, axis=1)
+        if mask:
+            part = lax.ppermute(part, "dev", [(d, d ^ mask) for d in range(ways)])
+        replies = lax.dynamic_update_slice_in_dim(replies, part, (here ^ mask) * height, axis=1)
     flat = replies.reshape(12, peers * width)
     return jnp.take(flat, owner * width + position, axis=1)
 

time: 149 us -> 157 us (1.054)
  starting transfers between devices: 20.9 us -> 25.8 us
  local copies, waits for them, and re-layouts: 93.4 us -> 97.9 us
  waiting for transfers between devices: 16 us -> 14 us
    ppermute x0 -> x7, starting transfers between devices: none -> 8.12 us  [lookup(): part = lax.ppermute(part, 'dev', [(d, d ^ mask) for d in range(ways)])]
    all_to_all x1 -> x0, waiting for transfers between devices: 5.68 us -> none  [lookup(): lax.all_to_all(found, 'dev', split_axis=1, concat_axis=1, tiled=True)]
    dynamic_update_slice x0 -> x8, local copies, waits for them, and re-layouts: none -> 4.84 us  [lookup(): lax.dynamic_update_slice_in_dim(replies, part, (here ^ mask) * height, ax...]
    all_to_all x1, waiting for transfers between devices: 1.76 us -> 5.47 us  [lookup(): lax.all_to_all(table, 'dev', split_axis=0, concat_axis=0, tiled=True)]
    all_to_all x1 -> x0, starting transfers between devices: 3.34 us -> none  [lookup(): lax.all_to_all(found, 'dev', split_axis=1, concat_axis=1, tiled=True)]
    unnamed x19 -> x17, local copies, waits for them, and re-layouts: 4.45 us -> 2.65 us
    gather x2 -> x1, local copies, waits for them, and re-layouts: 3.36 us -> 3.83 us  [lookup(): jnp.take(master_patch, lax.all_to_all(table, 'dev', split_axis=0, concat_...]
  transfers between devices with their start and end apart: 5 -> 11, of which waited for: 4 -> 3; matrix products, arithmetic and copies ran while one was open for 7% -> 9% of each run, Pallas kernels for 0% -> 0%
where the time goes in v1:
time: 157 us; the launch traced here: 154 us
  local copies, waits for them, and re-layouts  97.9 us (62%)
  starting transfers between devices  25.8 us (16%)
  other arithmetic  15.6 us (10%)
  waiting for transfers between devices  14 us (9%)
    scatter x1, local copies, waits for them, and re-layouts, lookup(): table = jnp.zeros((peers, width), jnp.int32).at[owner, position].set(offset)  76.9 us
    ppermute x7, starting transfers between devices, lookup(): part = lax.ppermute(part, 'dev', [(d, d ^ mask) for d in range(ways)])  8.12 us
    reduce_sum x1, other arithmetic, master_terms(): jnp.sum(paired * normals[:, direction][None, None], axis=-1).reshape(16, -1)  5.61 us
    all_to_all x1, waiting for transfers between devices, lookup(): lax.all_to_all(table, 'dev', split_axis=0, concat_axis=0, tiled=True)  5.47 us
    all_to_all x1, starting transfers between devices, local(): lax.all_to_all(owner_ids, 'zone', split_axis=0, concat_axis=0, tiled=True)  5.31 us
    all_to_all x1, starting transfers between devices, lookup(): lax.all_to_all(table, 'dev', split_axis=0, concat_axis=0, tiled=True)  4.88 us
    dynamic_update_slice x8, local copies, waits for them, and re-layouts, lookup(): lax.dynamic_update_slice_in_dim(replies, part, (here ^ mask) * height, ax...  4.84 us
    all_to_all x1, waiting for transfers between devices, local(): lax.all_to_all(found, 'zone', split_axis=1, concat_axis=1, tiled=True)  4.71 us
  transfers between devices with their start and end apart: 11, of which 3 were waited for; matrix products, arithmetic and copies ran while one was open for 9% of the time, Pallas kernels for 0%

profile of v1, /device:TPU:0, one launch (start us, length us, event | category | flops | bytes accessed | tf_op | source)
XLA Modules:
  0.0 154.2 jit_solution(824566327734965165)
XLA Ops:
  0.7 5.3 %all-to-all-start = ((s32[4,128,1]{1,2,0:T(1,128)}), s32[4,128,1]{1,2,0:T(1,128)S(1)}, u32[]{:S(2)}, u32[]{:S(2)}) async-start(s32[4,128,1]{1,2,0:T(1,128)} %bitcast.128), calls=%async_computation | async-start | bytes 4096 | tf_op jit(solution)/shard_map/all_to_all | solution.py:128
  6.0 3.4 %fusion.17 = (f32[512,1,128]{2,1,0:T(1,128)S(1)}, f32[512,1,128]{2,1,0:T(1,128)S(1)}, f32[512,1,128]{2,1,0:T(1,128)S(1)}, f32[512,1,128]{2,1,0:T(1,128)S(1)}) fusion(f32[512,4,128]{2,1,0:T(4,128)} %param.12), kind=kLoop, calls=%fused_computation.114 | loop fusion | bytes 2097152 | tf_op jit(solution)/shard_map/slice | solution.py:24
  9.4 1.2 slice_bitcast_fusion.1
  10.5 1.1 multiply_bitcast_fusion.3
  11.6 0.1 multiply_bitcast_fusion.7
  11.7 0.1 select_reduce_fusion.1
  11.8 2.6 %copy.66 = f32[12,8192]{0,1:T(8,128)} copy(f32[12,8192]{1,0:T(8,128)S(1)} %copy-done.2) | data formatting | bytes 786432 | tf_op args[10]
  14.4 4.2 %all-to-all-start.1 = ((s32[4,128,1]{1,2,0:T(1,128)}), s32[4,128,1]{1,2,0:T(1,128)S(1)}, u32[]{:S(2)}, u32[]{:S(2)}) async-start(s32[4,128,1]{1,2,0:T(1,128)} %bitcast.18), calls=%async_computation.1 | async-start | bytes 4096 | tf_op jit(solution)/shard_map/all_to_all | solution.py:129
  18.6 0.1 fusion.3
  18.7 0.3 reduce_window_sum.11
  19.0 0.2 select_reduce_fusion
  19.4 3.8 %all-to-all-done.1 = s32[4,128,1]{1,2,0:T(1,128)S(1)} async-done(((s32[4,128,1]{1,2,0:T(1,128)}), s32[4,128,1]{1,2,0:T(1,128)S(1)}, u32[]{:S(2)}, u32[]{:S(2)}) %all-to-all-start.1) | async-done | bytes 2080 | tf_op jit(solution)/shard_map/all_to_all | solution.py:129
  23.2 0.6 broadcast_in_dim.124
  23.8 76.9 %scatter_fusion = s32[8,64]{1,0:T(8,128)} fusion(s32[8,64]{1,0:T(8,128)} %broadcast_in_dim.124, s32[512]{0:T(512)S(1)} %bitcast.113, s32[512]{0:T(512)S(1)} %bitcast.125), kind=kCustom, calls=%fused_computation.2 | custom fusion | bytes 10240 | tf_op jit(solution)/shard_map/scatter | solution.py:90
  100.6 4.9 %all-to-all-start.2 = ((s32[8,1,64]{2,1,0:T(1,128)}), s32[8,1,64]{2,1,0:T(1,128)S(1)}, u32[]{:S(2)}, u32[]{:S(2)}) async-start(s32[8,1,64]{2,1,0:T(1,128)} %bitcast.21), calls=%async_computation.2 | async-start | bytes 8192 | tf_op jit(solution)/shard_map/all_to_all | solution.py:92
  105.5 5.5 %all-to-all-done.2 = s32[8,1,64]{2,1,0:T(1,128)S(1)} async-done(((s32[8,1,64]{2,1,0:T(1,128)}), s32[8,1,64]{2,1,0:T(1,128)S(1)}, u32[]{:S(2)}, u32[]{:S(2)}) %all-to-all-start.2) | async-done | bytes 2080 | tf_op jit(solution)/shard_map/all_to_all | solution.py:92
  111.0 0.1 reshape.572
  111.1 3.8 %gather_fusion = f32[512,12]{1,0:T(8,128)} fusion(f32[12,8192]{0,1:T(8,128)} %copy.66, s32[1024]{0:T(1024)S(1)} %pad_clamp_fusion.1), kind=kCustom, calls=%fused_computation | custom fusion | bytes 51200 | tf_op jit(solution)/shard_map/jit(_take)/gather | solution.py:91
  114.9 1.1 broadcast_select_fusion
  116.1 0.6 collective-permute-start.1
  116.8 1.2 collective-permute-start.2
  118.0 0.6 collective-permute-start.3
  118.6 2.0 %collective-permute-start.4 = (f32[12,1,64]{0,2,1:T(8,128)S(1)}, f32[12,1,64]{0,2,1:T(8,128)S(1)}, u32[]{:S(2)}, u32[]{:S(2)}) collective-permute-start(f32[12,1,64]{0,2,1:T(8,128)S(1)} %get-tuple-element.43), channel_id=1, source_target_pairs={{0,5},{1,4},{2,7},{3,6},{4,1},{5,0},{6,3},{7,2},{8,13},{9,12},{10,... | collective-permute-start | bytes 9224 | tf_op jit(solution)/shard_map/ppermute | solution.py:104
  120.6 0.7 broadcast_in_dim.123
  121.3 0.6 bitcast_dynamic-update-slice_fusion
  121.9 0.6 collective-permute-start.5
  122.5 0.6 constant_dynamic-update-slice_fusion.5
  123.1 3.0 %collective-permute-start.6 = (f32[12,1,64]{0,2,1:T(8,128)S(1)}, f32[12,1,64]{0,2,1:T(8,128)S(1)}, u32[]{:S(2)}, u32[]{:S(2)}) collective-permute-start(f32[12,1,64]{0,2,1:T(8,128)S(1)} %get-tuple-element.41), channel_id=1, source_target_pairs={{0,7},{1,6},{2,5},{3,4},{4,3},{5,2},{6,1},{7,0},{8,15},{9,14},{10,... | collective-permute-start | bytes 9224 | tf_op jit(solution)/shard_map/ppermute | solution.py:104
  126.1 0.6 constant_dynamic-update-slice_fusion.4
  126.7 0.6 constant_dynamic-update-slice_fusion.3
  127.3 0.6 constant_dynamic-update-slice_fusion.2
  127.9 0.6 constant_dynamic-update-slice_fusion.1
  128.6 0.6 constant_dynamic-update-slice_fusion
  129.2 0.6 constant_dynamic-update-slice_fusion.6
  129.8 2.6 %gather_fusion.1 = f32[512,12]{1,0:T(8,128)} fusion(f32[12,512]{0,1:T(8,128)} %bitcast.33, s32[1024]{0:T(1024)S(1)} %pad_clamp_fusion), kind=kCustom, calls=%fused_computation.1 | custom fusion | bytes 51200 | tf_op jit(solution)/shard_map/jit(_take)/gather | solution.py:107
  132.4 1.1 copy.67
  133.4 0.6 broadcast_select_fusion.1
  134.1 3.3 %all-to-all-start.3 = ((f32[12,4,128]{2,0,1:T(8,128)}), f32[12,4,128]{2,0,1:T(8,128)S(1)}, u32[]{:S(2)}, u32[]{:S(2)}) async-start(f32[12,4,128]{2,0,1:T(8,128)} %broadcast_select_fusion.1), calls=%async_computation.3 | async-start | bytes 65536 | tf_op jit(solution)/shard_map/all_to_all | solution.py:132
  137.3 4.7 %all-to-all-done.3 = f32[12,4,128]{2,0,1:T(8,128)S(1)} async-done(((f32[12,4,128]{2,0,1:T(8,128)}), f32[12,4,128]{2,0,1:T(8,128)S(1)}, u32[]{:S(2)}, u32[]{:S(2)}) %all-to-all-start.3) | async-done | bytes 24608 | tf_op jit(solution)/shard_map/all_to_all | solution.py:132
  142.1 2.2 %multiply_reduce_fusion.6 = (f32[512,128]{1,0:T(8,128)S(1)}, f32[512,128]{1,0:T(8,128)S(1)}, f32[512,128]{1,0:T(8,128)S(1)}, f32[4,512,128]{2,1,0:T(8,128)S(1)}) fusion(f32[4,512]{1,0:T(4,128)S(1)} %get-tuple-element.49, f32[1,512,128]{2,1,0:T(8,128)} %get-tuple-element.39, f32[1,512,128]{2,1,0:T(8,128)} %get-tuple-element.40, ...), kind=kLoop, calls=%fused_computation.17 | loop fusion | flops 2162688 | bytes 2908160 | tf_op jit(solution)/shard_map/reduce_sum | solution.py:37
  144.3 0.2 multiply_subtract_fusion.1
  144.5 0.1 multiply_subtract_fusion
  144.6 1.3 multiply_reduce_fusion.4
  145.9 0.6 maximum_divide_fusion
  146.5 0.6 fusion.4
  147.2 5.6 %fusion = (f32[4,4,512]{2,1,0:T(4,128)S(1)}, f32[4,4,512]{2,1,0:T(4,128)S(1)}, f32[4,4,512]{2,1,0:T(4,128)S(1)}, f32[4,4,512]{2,1,0:T(4,128)S(1)}, f32[4,4,512]{2,1,0:T(4,128)S(1)}) fusion(f32[512,128]{1,0:T(8,128)S(1)} %get-tuple-element.31, f32[4,512,128]{2,1,0:T(8,128)S(1)} %get-tuple-element.29, f32[4,512,128]{2,1,0:T(8,128)S(1)} %get-tuple-element.17, ...), kind=kLoop, calls=%fused_computation.7 | loop fusion | flops 10444800 | bytes 4096000 | tf_op jit(solution)/shard_map/reduce_sum | solution.py:46
  152.9 0.6 broadcast_select_fusion.2
  153.5 0.6 maximum_select_fusion
  (42 shorter events, 0.4 us)
Async XLA Ops:
  0.6 11.1 %copy-start.7 = (s32[1,4]{1,0:T(1,128)S(1)}, s32[1,4]{1,0:T(1,128)}, u32[]{:S(2)}) copy-start(s32[1,4]{1,0:T(1,128)} %param.17) | copy-start | bytes 52
  0.6 11.1 %copy-start.2 = (f32[12,8192]{1,0:T(8,128)S(1)}, f32[12,8192]{1,0:T(8,128)}, u32[]{:S(2)}) copy-start(f32[12,8192]{1,0:T(8,128)} %param.21) | copy-start | bytes 1179652
  0.7 13.8 %all-to-all-start = ((s32[4,128,1]{1,2,0:T(1,128)}), s32[4,128,1]{1,2,0:T(1,128)S(1)}, u32[]{:S(2)}, u32[]{:S(2)}) async-start(s32[4,128,1]{1,2,0:T(1,128)} %bitcast.128), calls=%async_computation | async-start | bytes 4096 | tf_op jit(solution)/shard_map/all_to_all | solution.py:128
  14.4 8.8 %all-to-all-start.1 = ((s32[4,128,1]{1,2,0:T(1,128)}), s32[4,128,1]{1,2,0:T(1,128)S(1)}, u32[]{:S(2)}, u32[]{:S(2)}) async-start(s32[4,128,1]{1,2,0:T(1,128)} %bitcast.18), calls=%async_computation.1 | async-start | bytes 4096 | tf_op jit(solution)/shard_map/all_to_all | solution.py:129
  23.8 120.5 %copy-start = (f32[512,3,128]{2,0,1:T(8,128)S(1)}, f32[512,3,128]{2,0,1:T(8,128)}, u32[]{:S(2)}) copy-start(f32[512,3,128]{2,0,1:T(8,128)} %param.14) | copy-start | bytes 2359300
  23.8 120.5 %copy-start.1 = (f32[512,3,128]{2,0,1:T(8,128)S(1)}, f32[512,3,128]{2,0,1:T(8,128)}, u32[]{:S(2)}) copy-start(f32[512,3,128]{2,0,1:T(8,128)} %param.13) | copy-start | bytes 2359300
  100.6 10.4 %all-to-all-start.2 = ((s32[8,1,64]{2,1,0:T(1,128)}), s32[8,1,64]{2,1,0:T(1,128)S(1)}, u32[]{:S(2)}, u32[]{:S(2)}) async-start(s32[8,1,64]{2,1,0:T(1,128)} %bitcast.21), calls=%async_computation.2 | async-start | bytes 8192 | tf_op jit(solution)/shard_map/all_to_all | solution.py:92
  116.1 5.9 %collective-permute-start = (f32[12,1,64]{0,2,1:T(8,128)S(1)}, f32[12,1,64]{0,2,1:T(8,128)S(1)}, u32[]{:S(2)}, u32[]{:S(2)}) collective-permute-start(f32[12,1,64]{0,2,1:T(8,128)S(1)} %get-tuple-element.47), channel_id=1, source_target_pairs={{0,1},{1,0},{2,3},{3,2},{4,5},{5,4},{6,7},{7,6},{8,9},{9,8},{10,11... | collective-permute-start | bytes 9224 | tf_op jit(solution)/shard_map/ppermute | solution.py:104
  116.1 6.9 %collective-permute-start.1 = (f32[12,1,64]{0,2,1:T(8,128)S(1)}, f32[12,1,64]{0,2,1:T(8,128)S(1)}, u32[]{:S(2)}, u32[]{:S(2)}) collective-permute-start(f32[12,1,64]{0,2,1:T(8,128)S(1)} %get-tuple-element.46), channel_id=1, source_target_pairs={{0,2},{1,3},{2,0},{3,1},{4,6},{5,7},{6,4},{7,5},{8,10},{9,11},{10,... | collective-permute-start | bytes 9224 | tf_op jit(solution)/shard_map/ppermute | solution.py:104
  116.8 9.9 %collective-permute-start.2 = (f32[12,1,64]{0,2,1:T(8,128)S(1)}, f32[12,1,64]{0,2,1:T(8,128)S(1)}, u32[]{:S(2)}, u32[]{:S(2)}) collective-permute-start(f32[12,1,64]{0,2,1:T(8,128)S(1)} %get-tuple-element.45), channel_id=1, source_target_pairs={{0,3},{1,2},{2,1},{3,0},{4,7},{5,6},{6,5},{7,4},{8,11},{9,10},{10,... | collective-permute-start | bytes 9224 | tf_op jit(solution)/shard_map/ppermute | solution.py:104
  118.0 9.3 %collective-permute-start.3 = (f32[12,1,64]{0,2,1:T(8,128)S(1)}, f32[12,1,64]{0,2,1:T(8,128)S(1)}, u32[]{:S(2)}, u32[]{:S(2)}) collective-permute-start(f32[12,1,64]{0,2,1:T(8,128)S(1)} %get-tuple-element.44), channel_id=1, source_target_pairs={{0,4},{1,5},{2,6},{3,7},{4,0},{5,1},{6,2},{7,3},{8,12},{9,13},{10,... | collective-permute-start | bytes 9224 | tf_op jit(solution)/shard_map/ppermute | solution.py:104
  118.6 9.4 %collective-permute-start.4 = (f32[12,1,64]{0,2,1:T(8,128)S(1)}, f32[12,1,64]{0,2,1:T(8,128)S(1)}, u32[]{:S(2)}, u32[]{:S(2)}) collective-permute-start(f32[12,1,64]{0,2,1:T(8,128)S(1)} %get-tuple-element.43), channel_id=1, source_target_pairs={{0,5},{1,4},{2,7},{3,6},{4,1},{5,0},{6,3},{7,2},{8,13},{9,12},{10,... | collective-permute-start | bytes 9224 | tf_op jit(solution)/shard_map/ppermute | solution.py:104
  121.9 6.6 %collective-permute-start.5 = (f32[12,1,64]{0,2,1:T(8,128)S(1)}, f32[12,1,64]{0,2,1:T(8,128)S(1)}, u32[]{:S(2)}, u32[]{:S(2)}) collective-permute-start(f32[12,1,64]{0,2,1:T(8,128)S(1)} %get-tuple-element.42), channel_id=1, source_target_pairs={{0,6},{1,7},{2,4},{3,5},{4,2},{5,3},{6,0},{7,1},{8,14},{9,15},{10,... | collective-permute-start | bytes 9224 | tf_op jit(solution)/shard_map/ppermute | solution.py:104
  123.1 6.1 %collective-permute-start.6 = (f32[12,1,64]{0,2,1:T(8,128)S(1)}, f32[12,1,64]{0,2,1:T(8,128)S(1)}, u32[]{:S(2)}, u32[]{:S(2)}) collective-permute-start(f32[12,1,64]{0,2,1:T(8,128)S(1)} %get-tuple-element.41), channel_id=1, source_target_pairs={{0,7},{1,6},{2,5},{3,4},{4,3},{5,2},{6,1},{7,0},{8,15},{9,14},{10,... | collective-permute-start | bytes 9224 | tf_op jit(solution)/shard_map/ppermute | solution.py:104
  134.1 8.0 %all-to-all-start.3 = ((f32[12,4,128]{2,0,1:T(8,128)}), f32[12,4,128]{2,0,1:T(8,128)S(1)}, u32[]{:S(2)}, u32[]{:S(2)}) async-start(f32[12,4,128]{2,0,1:T(8,128)} %broadcast_select_fusion.1), calls=%async_computation.3 | async-start | bytes 65536 | tf_op jit(solution)/shard_map/all_to_all | solution.py:132
  142.1 2.6 %copy-start.3 = (f32[512,128]{1,0:T(8,128)S(1)}, f32[512,128]{1,0:T(8,128)}, u32[]{:S(2)}) copy-start(f32[512,128]{1,0:T(8,128)} %param.11) | copy-start | bytes 786436
  144.3 1.6 %copy-start.4 = (f32[12,512]{1,0:T(8,128)S(1)}, f32[12,512]{1,0:T(8,128)}, u32[]{:S(2)}) copy-start(f32[12,512]{1,0:T(8,128)} %param.20) | copy-start | bytes 73732
  144.5 1.5 copy-start.5
  144.5 1.5 copy-start.6
